TPU v7x, 256 devices: a whole 4x4x8 slice. The times are simulated.
256 devices in a mesh: chain: 64 (over z, y, core), col: 4 (over x).
Axes of the slice: x: 4, y: 4, z: 8, core: 2. Of those that a mesh axis runs over, the one named last changes fastest.
Arguments:
- diagonal_blocks: float32 [192, 256, 256], P('chain', 'col'), may hold values from -2 to 6, as said below
- couplings: float32 [192, 256, 256], P('chain', 'col'), may hold values from -2 to 2
- right_sides: float32 [64, 192, 256], P('col', 'chain'), may hold values from -0.04 to 0.04
Outputs:
- solution: float32 [64, 192, 256], P('col', 'chain')
Inputs may be any that keep to these rules, and one draw needn't show every extreme that they name: `diagonal_blocks`: each block is symmetric, and the block-tridiagonal matrix that the diagonal blocks form with the couplings is positive definite with every eigenvalue 0.0003 or more.
All inputs are finite; a program needn't handle non-finite values.
Results may differ from a plain program's by a relative error of at most 0.0003.
Values sent between devices are 32-bit elements; how exact they have to be, the bound alone decides.
A program may use at most 64 MiB of HBM per device.

v0:
```python
import jax
import jax.numpy as jnp
from jax import lax
from jax.sharding import PartitionSpec as P

finest = lax.Precision.HIGHEST


def passed_along(shard, axis, by):
    size = lax.axis_size(axis)
    pairs = [(i, i + by) for i in range(size) if 0 <= i + by < size]
    return lax.ppermute(shard, axis, pairs)


def matmul(first_factor, second_factor):
    return jnp.dot(first_factor, second_factor, precision=finest)


def invert(matrix):
    lower_factor = jnp.linalg.cholesky(matrix)
    identity = jnp.eye(matrix.shape[0], dtype=matrix.dtype)
    return jax.scipy.linalg.cho_solve((lower_factor, True), identity)


def interior_solve(loads, inverses, products, inner_coups):
    before = jnp.concatenate([jnp.zeros_like(inner_coups), inner_coups], axis=0)

    def interior_forward(solved_prev, entries):
        load_now, coup_prev, inverse_now = entries
        reduced = load_now - matmul(solved_prev, coup_prev)
        solved_now = matmul(reduced, inverse_now.T)
        return (solved_now, solved_now)

    _, solved = lax.scan(interior_forward, jnp.zeros_like(loads[0]), (loads, before, inverses))

    def interior_backward(after, entries):
        solved_now, product = entries
        current = solved_now - matmul(after, product.T)
        return (current, current)

    _, earlier = lax.scan(interior_backward, solved[-1], (solved[:-1], products), reverse=True)
    return jnp.concatenate([earlier, solved[-1:]], axis=0)


def per_device(diagonal_blocks, couplings, right_sides):
    slab_count = diagonal_blocks.shape[0]
    col_width = diagonal_blocks.shape[1]
    inner_count = slab_count - 1
    col_start = lax.axis_index("col") * col_width
    chain_count = lax.axis_size("chain")
    levels = chain_count.bit_length() - 1
    full_diag, full_coup = (
        lax.all_gather(diagonal_blocks[:inner_count], "col", axis=1, tiled=True),
        lax.all_gather(couplings, "col", axis=1, tiled=True),
    )

    def body_forward(inverse_prev, entries):
        diag_now, coup_prev = entries
        product = matmul(inverse_prev, coup_prev)
        inverse_now = invert(diag_now - matmul(coup_prev.T, product))
        return (inverse_now, (inverse_prev, product))

    last_inverse, (early_inverses, products) = lax.scan(
        body_forward, invert(full_diag[0]), (full_diag[1:], full_coup[: inner_count - 1])
    )
    inverses = jnp.concatenate([early_inverses, last_inverse[None]], axis=0)
    inner_coups = full_coup[: inner_count - 1]
    coup_last = full_coup[inner_count - 1]
    coup_sep = full_coup[inner_count]
    last_cols = lax.dynamic_slice_in_dim(coup_last, col_start, col_width, 1)
    tail_start = matmul(last_inverse, last_cols)

    def body_backward(state, entries):
        green_block, tail_block = state
        inverse_now, product = entries
        green_block = inverse_now + matmul(matmul(product, green_block), product.T)
        tail_block = -matmul(product, tail_block)
        return ((green_block, tail_block), None)

    (near_green, near_tail), _ = lax.scan(
        body_backward, (last_inverse, tail_start), (early_inverses, products), reverse=True
    )
    loads = jnp.swapaxes(right_sides, 0, 1)
    interior = interior_solve(loads[:inner_count], inverses, products, inner_coups)
    got_green, got_tail, got_first = passed_along((near_green, near_tail, interior[0]), "chain", -1)
    sep_rows = lax.dynamic_slice_in_dim(coup_sep, col_start, col_width, 0)
    own_block = diagonal_blocks[inner_count].T
    b_part = (
        own_block
        - matmul(coup_last.T, tail_start)
        - matmul(coup_sep, matmul(got_green, sep_rows.T))
    )
    c_part = -matmul(coup_sep, got_tail)
    h_part = (
        loads[inner_count]
        - matmul(interior[inner_count - 1], coup_last)
        - matmul(got_first, coup_sep.T)
    )
    for level_index in range(levels):
        distance = 1 << level_index
        b_full, c_full = (
            lax.all_gather(b_part, "col", axis=1, tiled=True),
            lax.all_gather(c_part, "col", axis=1, tiled=True),
        )
        inverse = invert(b_full)
        coupling_rows = lax.dynamic_slice_in_dim(c_full, col_start, col_width, 0)
        solved_cols = matmul(inverse, c_part)
        solved_loads = matmul(h_part, inverse.T)
        below_blocks, below_loads = passed_along(
            (matmul(c_full.T, solved_cols), matmul(solved_loads, c_full)), "chain", distance
        )
        far_inverse, far_cols, far_loads = passed_along(
            (inverse, solved_cols, solved_loads), "chain", -distance
        )
        b_part = b_part - below_blocks - matmul(c_full, matmul(far_inverse, coupling_rows.T))
        c_part = -matmul(c_full, far_cols)
        h_part = h_part - below_loads - matmul(far_loads, c_full.T)
    b_final = lax.all_gather(b_part, "col", axis=1, tiled=True)
    separator = jax.scipy.linalg.cho_solve((jnp.linalg.cholesky(b_final), True), h_part.T).T
    carried = passed_along(matmul(separator, coup_sep), "chain", 1)
    adjusted = loads[:inner_count]
    adjusted = adjusted.at[0].add(-carried)
    adjusted = adjusted.at[inner_count - 1].add(-matmul(separator, coup_last.T))
    solved_inner = interior_solve(adjusted, inverses, products, inner_coups)
    return jnp.swapaxes(jnp.concatenate([solved_inner, separator[None]], axis=0), 0, 1)


def solution(mesh):
    in_specs = (P("chain", "col", None), P("chain", "col", None), P("col", "chain", None))
    out_specs = P("col", "chain", None)
    return jax.shard_map(
        per_device, mesh=mesh, in_specs=in_specs, out_specs=out_specs, check_vma=False
    )
```

profile of v0, /device:TPU:250, one launch (start us, length us, event | category | flops | bytes accessed | tf_op | source)
XLA Modules:
  0.0 923.8 jit_solution(14875295477138087786)
XLA Ops:
  1.0 13.5 %all_gather.45 = f32[2,256,256]{2,0,1:T(2,128)S(1)} all-gather(f32[2,64,256]{2,0,1:T(2,128)S(1)} %copy.26), channel_id=1, replica_groups=mesh['chain'=64,'col'=4] {'col'}, dimensions={1}, use_global_device_ids=true | all-gather | bytes 655360 | tf_op jit(solution)/shard_map/all_gather | solution.py:53
  15.1 11.7 %cholesky.424 = f32[128,128]{1,0:T(8,128)S(1)} custom-call(f32[128,128]{1,0:T(8,128)S(1)} %cholesky.726), custom_call_target="Cholesky" | custom-call | tf_op jit(solution)/shard_map/jit(cholesky)/cholesky | solution.py:20
  26.9 9.8 %custom-call.36 = f32[1,128,128]{1,2,0:T(8,128)S(1)} custom-call(f32[1,128,128]{2,1,0:T(8,128)S(1)} %get-tuple-element.384), custom_call_target="InvertDiagBlocksLowerTriangular" | custom-call | tf_op jit(solution)/shard_map/jit(cholesky)/cholesky | solution.py:20
  37.2 11.7 %cholesky.441 = f32[128,128]{1,0:T(8,128)S(1)} custom-call(f32[128,128]{1,0:T(8,128)S(1)} %convolution_subtract_fusion.24), custom_call_target="Cholesky" | custom-call | tf_op jit(solution)/shard_map/jit(cholesky)/cholesky | solution.py:20
  55.0 19.7 %custom-call.37 = f32[2,128,128]{1,2,0:T(8,128)S(1)} custom-call(f32[2,128,128]{2,1,0:T(8,128)S(1)} %get-tuple-element.218), custom_call_target="InvertDiagBlocksLowerTriangular" | custom-call | tf_op jit(solution)/shard_map/jit(_cho_solve)/triangular_solve | solution.py:22
  77.1 14.0 %all_gather.46 = f32[3,256,256]{2,1,0:T(8,128)S(1)} all-gather(f32[3,64,256]{2,1,0:T(8,128)S(1)} %copy-done.19), channel_id=1, replica_groups=mesh['chain'=64,'col'=4] {'col'}, dimensions={1}, use_global_device_ids=true | all-gather | bytes 983040 | tf_op jit(solution)/shard_map/all_gather | solution.py:54
  93.3 11.7 %cholesky.458 = f32[128,128]{1,0:T(8,128)S(1)} custom-call(f32[128,128]{1,0:T(8,128)S(1)} %cholesky.729), custom_call_target="Cholesky" | custom-call | tf_op jit(solution)/shard_map/while/body/eval_jaxpr/jit(cholesky)/cholesky | solution.py:20
  105.0 9.8 %custom-call.38 = f32[1,128,128]{1,2,0:T(8,128)S(1)} custom-call(f32[1,128,128]{2,1,0:T(8,128)S(1)} %get-tuple-element.380), custom_call_target="InvertDiagBlocksLowerTriangular" | custom-call | tf_op jit(solution)/shard_map/while/body/eval_jaxpr/jit(cholesky)/cholesky | solution.py:20
  115.3 11.7 %cholesky.475 = f32[128,128]{1,0:T(8,128)S(1)} custom-call(f32[128,128]{1,0:T(8,128)S(1)} %convolution_subtract_fusion.23), custom_call_target="Cholesky" | custom-call | tf_op jit(solution)/shard_map/while/body/eval_jaxpr/jit(cholesky)/cholesky | solution.py:20
  133.8 19.7 %custom-call.39 = f32[2,128,128]{1,2,0:T(8,128)S(1)} custom-call(f32[2,128,128]{2,1,0:T(8,128)S(1)} %get-tuple-element.219), custom_call_target="InvertDiagBlocksLowerTriangular" | custom-call | tf_op jit(solution)/shard_map/while/body/eval_jaxpr/jit(_cho_solve)/triangular_solve | solution.py:22
  170.3 12.3 %all_gather.47 = f32[256,256]{0,1:T(8,128)S(1)} all-gather(f32[256,64]{0,1:T(8,128)S(1)} %bitcast.554), channel_id=1, replica_groups=mesh['chain'=64,'col'=4] {'col'}, dimensions={1}, use_global_device_ids=true | all-gather | bytes 327680 | tf_op jit(solution)/shard_map/all_gather | solution.py:103
  185.6 12.7 %all_gather.48 = f32[256,256]{0,1:T(8,128)S(1)} all-gather(f32[256,64]{0,1:T(8,128)S(1)} %fusion.17), channel_id=1, replica_groups=mesh['chain'=64,'col'=4] {'col'}, dimensions={1}, use_global_device_ids=true | all-gather | bytes 327680 | tf_op jit(solution)/shard_map/all_gather | solution.py:102
  198.6 11.7 %cholesky.492 = f32[128,128]{1,0:T(8,128)S(1)} custom-call(f32[128,128]{1,0:T(8,128)S(1)} %cholesky.732), custom_call_target="Cholesky" | custom-call | tf_op jit(solution)/shard_map/jit(cholesky)/cholesky | solution.py:20
  210.3 9.8 %custom-call.40 = f32[1,128,128]{1,2,0:T(8,128)S(1)} custom-call(f32[1,128,128]{2,1,0:T(8,128)S(1)} %get-tuple-element.376), custom_call_target="InvertDiagBlocksLowerTriangular" | custom-call | tf_op jit(solution)/shard_map/jit(cholesky)/cholesky | solution.py:20
  220.6 11.7 %cholesky.509 = f32[128,128]{1,0:T(8,128)S(1)} custom-call(f32[128,128]{1,0:T(8,128)S(1)} %convolution_subtract_fusion.22), custom_call_target="Cholesky" | custom-call | tf_op jit(solution)/shard_map/jit(cholesky)/cholesky | solution.py:20
  240.0 19.7 %custom-call.41 = f32[2,128,128]{1,2,0:T(8,128)S(1)} custom-call(f32[2,128,128]{2,1,0:T(8,128)S(1)} %get-tuple-element.220), custom_call_target="InvertDiagBlocksLowerTriangular" | custom-call | tf_op jit(solution)/shard_map/jit(_cho_solve)/triangular_solve | solution.py:22
  276.8 12.2 %all_gather.49 = f32[256,256]{0,1:T(8,128)S(1)} all-gather(f32[256,64]{0,1:T(8,128)S(1)} %convolution_negate_fusion.5), channel_id=1, replica_groups=mesh['chain'=64,'col'=4] {'col'}, dimensions={1}, use_global_device_ids=true | all-gather | bytes 327680 | tf_op jit(solution)/shard_map/all_gather | solution.py:103
  290.3 12.3 %all_gather.50 = f32[256,256]{0,1:T(8,128)S(1)} all-gather(f32[256,64]{0,1:T(8,128)S(1)} %subtract_subtract_fusion.5), channel_id=1, replica_groups=mesh['chain'=64,'col'=4] {'col'}, dimensions={1}, use_global_device_ids=true | all-gather | bytes 327680 | tf_op jit(solution)/shard_map/all_gather | solution.py:102
  302.7 11.7 %cholesky.526 = f32[128,128]{1,0:T(8,128)S(1)} custom-call(f32[128,128]{1,0:T(8,128)S(1)} %cholesky.735), custom_call_target="Cholesky" | custom-call | tf_op jit(solution)/shard_map/jit(cholesky)/cholesky | solution.py:20
  314.5 9.8 %custom-call.42 = f32[1,128,128]{1,2,0:T(8,128)S(1)} custom-call(f32[1,128,128]{2,1,0:T(8,128)S(1)} %get-tuple-element.372), custom_call_target="InvertDiagBlocksLowerTriangular" | custom-call | tf_op jit(solution)/shard_map/jit(cholesky)/cholesky | solution.py:20
  324.8 11.7 %cholesky.543 = f32[128,128]{1,0:T(8,128)S(1)} custom-call(f32[128,128]{1,0:T(8,128)S(1)} %convolution_subtract_fusion.21), custom_call_target="Cholesky" | custom-call | tf_op jit(solution)/shard_map/jit(cholesky)/cholesky | solution.py:20
  339.2 5.7 while.70
  344.9 19.7 %custom-call.43 = f32[2,128,128]{1,2,0:T(8,128)S(1)} custom-call(f32[2,128,128]{2,1,0:T(8,128)S(1)} %get-tuple-element.221), custom_call_target="InvertDiagBlocksLowerTriangular" | custom-call | tf_op jit(solution)/shard_map/jit(_cho_solve)/triangular_solve | solution.py:22
  372.5 5.7 collective-permute-start.7
  384.7 12.3 %all_gather.51 = f32[256,256]{0,1:T(8,128)S(1)} all-gather(f32[256,64]{0,1:T(8,128)S(1)} %convolution_negate_fusion.4), channel_id=1, replica_groups=mesh['chain'=64,'col'=4] {'col'}, dimensions={1}, use_global_device_ids=true | all-gather | bytes 327680 | tf_op jit(solution)/shard_map/all_gather | solution.py:103
  398.5 12.2 %all_gather.52 = f32[256,256]{0,1:T(8,128)S(1)} all-gather(f32[256,64]{0,1:T(8,128)S(1)} %subtract_subtract_fusion.4), channel_id=1, replica_groups=mesh['chain'=64,'col'=4] {'col'}, dimensions={1}, use_global_device_ids=true | all-gather | bytes 327680 | tf_op jit(solution)/shard_map/all_gather | solution.py:102
  410.9 11.7 %cholesky.560 = f32[128,128]{1,0:T(8,128)S(1)} custom-call(f32[128,128]{1,0:T(8,128)S(1)} %cholesky.738), custom_call_target="Cholesky" | custom-call | tf_op jit(solution)/shard_map/jit(cholesky)/cholesky | solution.py:20
  422.7 9.8 %custom-call.44 = f32[1,128,128]{1,2,0:T(8,128)S(1)} custom-call(f32[1,128,128]{2,1,0:T(8,128)S(1)} %get-tuple-element.368), custom_call_target="InvertDiagBlocksLowerTriangular" | custom-call | tf_op jit(solution)/shard_map/jit(cholesky)/cholesky | solution.py:20
  433.0 11.7 %cholesky.577 = f32[128,128]{1,0:T(8,128)S(1)} custom-call(f32[128,128]{1,0:T(8,128)S(1)} %convolution_subtract_fusion.20), custom_call_target="Cholesky" | custom-call | tf_op jit(solution)/shard_map/jit(cholesky)/cholesky | solution.py:20
  451.8 19.7 %custom-call.45 = f32[2,128,128]{1,2,0:T(8,128)S(1)} custom-call(f32[2,128,128]{2,1,0:T(8,128)S(1)} %get-tuple-element.222), custom_call_target="InvertDiagBlocksLowerTriangular" | custom-call | tf_op jit(solution)/shard_map/jit(_cho_solve)/triangular_solve | solution.py:22
  474.5 7.2 collective-permute-start.25
  483.0 4.9 collective-permute-start.10
  489.2 6.1 collective-permute-start.9
  497.7 12.3 %all_gather.53 = f32[256,256]{0,1:T(8,128)S(1)} all-gather(f32[256,64]{0,1:T(8,128)S(1)} %convolution_negate_fusion.3), channel_id=1, replica_groups=mesh['chain'=64,'col'=4] {'col'}, dimensions={1}, use_global_device_ids=true | all-gather | bytes 327680 | tf_op jit(solution)/shard_map/all_gather | solution.py:103
  511.2 12.3 %all_gather.54 = f32[256,256]{0,1:T(8,128)S(1)} all-gather(f32[256,64]{0,1:T(8,128)S(1)} %subtract_subtract_fusion.3), channel_id=1, replica_groups=mesh['chain'=64,'col'=4] {'col'}, dimensions={1}, use_global_device_ids=true | all-gather | bytes 327680 | tf_op jit(solution)/shard_map/all_gather | solution.py:102
  523.6 11.7 %cholesky.594 = f32[128,128]{1,0:T(8,128)S(1)} custom-call(f32[128,128]{1,0:T(8,128)S(1)} %cholesky.741), custom_call_target="Cholesky" | custom-call | tf_op jit(solution)/shard_map/jit(cholesky)/cholesky | solution.py:20
  535.4 9.8 %custom-call.46 = f32[1,128,128]{1,2,0:T(8,128)S(1)} custom-call(f32[1,128,128]{2,1,0:T(8,128)S(1)} %get-tuple-element.364), custom_call_target="InvertDiagBlocksLowerTriangular" | custom-call | tf_op jit(solution)/shard_map/jit(cholesky)/cholesky | solution.py:20
  545.7 11.7 %cholesky.611 = f32[128,128]{1,0:T(8,128)S(1)} custom-call(f32[128,128]{1,0:T(8,128)S(1)} %convolution_subtract_fusion.19), custom_call_target="Cholesky" | custom-call | tf_op jit(solution)/shard_map/jit(cholesky)/cholesky | solution.py:20
  560.0 5.5 while.72
  565.5 19.7 %custom-call.47 = f32[2,128,128]{1,2,0:T(8,128)S(1)} custom-call(f32[2,128,128]{2,1,0:T(8,128)S(1)} %get-tuple-element.223), custom_call_target="InvertDiagBlocksLowerTriangular" | custom-call | tf_op jit(solution)/shard_map/jit(_cho_solve)/triangular_solve | solution.py:22
  588.5 5.9 collective-permute-start.27
  606.4 12.2 %all_gather.55 = f32[256,256]{0,1:T(8,128)S(1)} all-gather(f32[256,64]{0,1:T(8,128)S(1)} %convolution_negate_fusion.2), channel_id=1, replica_groups=mesh['chain'=64,'col'=4] {'col'}, dimensions={1}, use_global_device_ids=true | all-gather | bytes 327680 | tf_op jit(solution)/shard_map/all_gather | solution.py:103
  620.1 12.2 %all_gather.56 = f32[256,256]{0,1:T(8,128)S(1)} all-gather(f32[256,64]{0,1:T(8,128)S(1)} %subtract_subtract_fusion.2), channel_id=1, replica_groups=mesh['chain'=64,'col'=4] {'col'}, dimensions={1}, use_global_device_ids=true | all-gather | bytes 327680 | tf_op jit(solution)/shard_map/all_gather | solution.py:102
  632.6 11.7 %cholesky.628 = f32[128,128]{1,0:T(8,128)S(1)} custom-call(f32[128,128]{1,0:T(8,128)S(1)} %cholesky.744), custom_call_target="Cholesky" | custom-call | tf_op jit(solution)/shard_map/jit(cholesky)/cholesky | solution.py:20
  644.4 9.8 %custom-call.48 = f32[1,128,128]{1,2,0:T(8,128)S(1)} custom-call(f32[1,128,128]{2,1,0:T(8,128)S(1)} %get-tuple-element.360), custom_call_target="InvertDiagBlocksLowerTriangular" | custom-call | tf_op jit(solution)/shard_map/jit(cholesky)/cholesky | solution.py:20
  654.6 11.7 %cholesky.645 = f32[128,128]{1,0:T(8,128)S(1)} custom-call(f32[128,128]{1,0:T(8,128)S(1)} %convolution_subtract_fusion.18), custom_call_target="Cholesky" | custom-call | tf_op jit(solution)/shard_map/jit(cholesky)/cholesky | solution.py:20
  673.8 19.7 %custom-call.49 = f32[2,128,128]{1,2,0:T(8,128)S(1)} custom-call(f32[2,128,128]{2,1,0:T(8,128)S(1)} %get-tuple-element.224), custom_call_target="InvertDiagBlocksLowerTriangular" | custom-call | tf_op jit(solution)/shard_map/jit(_cho_solve)/triangular_solve | solution.py:22
  696.5 9.1 collective-permute-start.29
  712.8 5.5 collective-permute-start.15
  720.7 12.2 %all_gather.57 = f32[256,256]{0,1:T(8,128)S(1)} all-gather(f32[256,64]{0,1:T(8,128)S(1)} %convolution_negate_fusion.1), channel_id=1, replica_groups=mesh['chain'=64,'col'=4] {'col'}, dimensions={1}, use_global_device_ids=true | all-gather | bytes 327680 | tf_op jit(solution)/shard_map/all_gather | solution.py:103
  734.2 12.3 %all_gather.58 = f32[256,256]{0,1:T(8,128)S(1)} all-gather(f32[256,64]{0,1:T(8,128)S(1)} %subtract_subtract_fusion.1), channel_id=1, replica_groups=mesh['chain'=64,'col'=4] {'col'}, dimensions={1}, use_global_device_ids=true | all-gather | bytes 327680 | tf_op jit(solution)/shard_map/all_gather | solution.py:102
  746.6 11.7 %cholesky.662 = f32[128,128]{1,0:T(8,128)S(1)} custom-call(f32[128,128]{1,0:T(8,128)S(1)} %cholesky.747), custom_call_target="Cholesky" | custom-call | tf_op jit(solution)/shard_map/jit(cholesky)/cholesky | solution.py:20
  758.4 9.8 %custom-call.50 = f32[1,128,128]{1,2,0:T(8,128)S(1)} custom-call(f32[1,128,128]{2,1,0:T(8,128)S(1)} %get-tuple-element.356), custom_call_target="InvertDiagBlocksLowerTriangular" | custom-call | tf_op jit(solution)/shard_map/jit(cholesky)/cholesky | solution.py:20
  768.7 11.7 %cholesky.679 = f32[128,128]{1,0:T(8,128)S(1)} custom-call(f32[128,128]{1,0:T(8,128)S(1)} %convolution_subtract_fusion.17), custom_call_target="Cholesky" | custom-call | tf_op jit(solution)/shard_map/jit(cholesky)/cholesky | solution.py:20
  783.3 5.9 while.74
  789.2 19.7 %custom-call.51 = f32[2,128,128]{1,2,0:T(8,128)S(1)} custom-call(f32[2,128,128]{2,1,0:T(8,128)S(1)} %get-tuple-element.225), custom_call_target="InvertDiagBlocksLowerTriangular" | custom-call | tf_op jit(solution)/shard_map/jit(_cho_solve)/triangular_solve | solution.py:22
  811.9 7.3 collective-permute-start.31
  820.8 8.5 collective-permute-start.18
  833.6 6.1 collective-permute-done.17
  840.2 12.3 %all_gather.59 = f32[256,256]{0,1:T(8,128)S(1)} all-gather(f32[256,64]{0,1:T(8,128)S(1)} %subtract_subtract_fusion), channel_id=1, replica_groups=mesh['chain'=64,'col'=4] {'col'}, dimensions={1}, use_global_device_ids=true | all-gather | bytes 327680 | tf_op jit(solution)/shard_map/all_gather | solution.py:118
  852.6 11.7 %cholesky.696 = f32[128,128]{1,0:T(8,128)S(1)} custom-call(f32[128,128]{1,0:T(8,128)S(1)} %cholesky.750), custom_call_target="Cholesky" | custom-call | tf_op jit(solution)/shard_map/jit(cholesky)/cholesky | solution.py:119
  864.4 9.8 %custom-call.52 = f32[1,128,128]{1,2,0:T(8,128)S(1)} custom-call(f32[1,128,128]{2,1,0:T(8,128)S(1)} %get-tuple-element.352), custom_call_target="InvertDiagBlocksLowerTriangular" | custom-call | tf_op jit(solution)/shard_map/jit(cholesky)/cholesky | solution.py:119
  874.7 11.7 %cholesky.713 = f32[128,128]{1,0:T(8,128)S(1)} custom-call(f32[128,128]{1,0:T(8,128)S(1)} %convolution_subtract_fusion.16), custom_call_target="Cholesky" | custom-call | tf_op jit(solution)/shard_map/jit(cholesky)/cholesky | solution.py:119
  893.8 19.7 %custom-call.20 = f32[2,128,128]{1,2,0:T(8,128)S(1)} custom-call(f32[2,128,128]{2,1,0:T(8,128)S(1)} %get-tuple-element.175), custom_call_target="InvertDiagBlocksLowerTriangular" | custom-call | tf_op jit(solution)/shard_map/jit(_cho_solve)/triangular_solve | solution.py:119
  (440 shorter events, 204.5 us)
Async XLA Ops:
  0.0 0.9 slice-start
  76.1 0.9 copy-start.19
  133.8 20.0 %copy-start.26 = (s32[2,2]{1,0:T(2,128)}, s32[2,2]{1,0:T(2,128)S(1)}, u32[]{:S(2)}) copy-start(s32[2,2]{1,0:T(2,128)S(1)} %get-tuple-element.999) | copy-start | bytes 52
  155.2 0.8 copy-start.20
  158.3 10.2 %collective-permute-start.19 = (f32[16,256]{1,0:T(8,128)}, f32[16,256]{1,0:T(8,128)S(1)}, u32[]{:S(2)}, u32[]{:S(2)}) collective-permute-start(f32[16,256]{1,0:T(8,128)} %convolution_subtract_fusion.29), channel_id=1, source_target_pairs={{4,0},{8,4},{12,8},{16,12},{20,16},{24,20},{28,24},{32,28},{36,32}... | collective-permute-start | bytes 49160 | tf_op jit(solution)/shard_map/ppermute | solution.py:12
  160.6 3.9 copy-start.16
  161.7 20.9 %collective-permute-start = (f32[256,256]{1,0:T(8,128)}, f32[256,256]{1,0:T(8,128)S(1)}, u32[]{:S(2)}, u32[]{:S(2)}) collective-permute-start(f32[256,256]{1,0:T(8,128)} %convolution_add_fusion), channel_id=1, source_target_pairs={{4,0},{8,4},{12,8},{16,12},{20,16},{24,20},{28,24},{32,28},{36,32}... | collective-permute-start | bytes 786440 | tf_op jit(solution)/shard_map/ppermute | solution.py:12
  164.9 2.3 copy-start.17
  165.3 4.6 collective-permute-start.1
  182.6 0.7 copy-start.18
  185.0 0.6 copy-start.6
  235.1 0.7 copy-start.27
  262.1 13.5 %collective-permute-start.21 = (f32[16,256]{1,0:T(8,128)S(1)}, f32[16,256]{1,0:T(8,128)S(1)}, u32[]{:S(2)}, u32[]{:S(2)}) collective-permute-start(f32[16,256]{1,0:T(8,128)S(1)} %fusion.228), channel_id=1, source_target_pairs={{4,0},{8,4},{12,8},{16,12},{20,16},{24,20},{28,24},{32,28},{36,32}... | collective-permute-start | bytes 49160 | tf_op jit(solution)/shard_map/ppermute | solution.py:12
  265.4 10.4 %collective-permute-start.4 = (f32[256,64]{0,1:T(8,128)S(1)}, f32[256,64]{0,1:T(8,128)S(1)}, u32[]{:S(2)}, u32[]{:S(2)}) collective-permute-start(f32[256,64]{0,1:T(8,128)S(1)} %fusion.229), channel_id=1, source_target_pairs={{4,0},{8,4},{12,8},{16,12},{20,16},{24,20},{28,24},{32,28},{36,32}... | collective-permute-start | bytes 196616 | tf_op jit(solution)/shard_map/ppermute | solution.py:12
  268.1 99.2 %collective-permute-start.20 = (f32[16,256]{1,0:T(8,128)}, f32[16,256]{1,0:T(8,128)S(1)}, u32[]{:S(2)}, u32[]{:S(2)}) collective-permute-start(f32[16,256]{1,0:T(8,128)} %fusion.247), channel_id=1, source_target_pairs={{0,4},{4,8},{8,12},{12,16},{16,20},{20,24},{24,28},{28,32},{32,36}... | collective-permute-start | bytes 49160 | tf_op jit(solution)/shard_map/ppermute | solution.py:12
  270.1 19.0 %collective-permute-start.3 = (f32[256,256]{1,0:T(8,128)S(1)}, f32[256,256]{1,0:T(8,128)S(1)}, u32[]{:S(2)}, u32[]{:S(2)}) collective-permute-start(f32[256,256]{1,0:T(8,128)S(1)} %pad_maximum_fusion.3), channel_id=1, source_target_pairs={{4,0},{8,4},{12,8},{16,12},{20,16},{24,20},{28,24},{32,28},{36,32}... | collective-permute-start | bytes 786440 | tf_op jit(solution)/shard_map/ppermute | solution.py:12
  273.7 15.8 %collective-permute-start.2 = (f32[256,64]{0,1:T(8,128)S(1)}, f32[256,64]{0,1:T(8,128)S(1)}, u32[]{:S(2)}, u32[]{:S(2)}) collective-permute-start(f32[256,64]{0,1:T(8,128)S(1)} %fusion.241), channel_id=1, source_target_pairs={{0,4},{4,8},{8,12},{12,16},{16,20},{20,24},{24,28},{28,32},{32,36}... | collective-permute-start | bytes 196616 | tf_op jit(solution)/shard_map/ppermute | solution.py:12
  276.2 0.6 copy-start.8
  289.0 0.8 copy-start.7
  366.1 0.8 copy-start.9
  367.3 0.6 copy-start.21
  367.9 16.2 %collective-permute-start.23 = (f32[16,256]{1,0:T(8,128)S(1)}, f32[16,256]{1,0:T(8,128)S(1)}, u32[]{:S(2)}, u32[]{:S(2)}) collective-permute-start(f32[16,256]{1,0:T(8,128)S(1)} %fusion.209), channel_id=1, source_target_pairs={{8,0},{12,4},{16,8},{20,12},{24,16},{28,20},{32,24},{36,28},{40,32... | collective-permute-start | bytes 49160 | tf_op jit(solution)/shard_map/ppermute | solution.py:12
  370.8 13.4 %collective-permute-start.22 = (f32[16,256]{1,0:T(8,128)S(1)}, f32[16,256]{1,0:T(8,128)S(1)}, u32[]{:S(2)}, u32[]{:S(2)}) collective-permute-start(f32[16,256]{1,0:T(8,128)S(1)} %fusion.249), channel_id=1, source_target_pairs={{0,8},{4,12},{8,16},{12,20},{16,24},{20,28},{24,32},{28,36},{32,40... | collective-permute-start | bytes 49160 | tf_op jit(solution)/shard_map/ppermute | solution.py:12
  372.5 11.7 %copy-start.22 = (f32[16,256]{1,0:T(8,128)S(1)}, f32[16,256]{1,0:T(8,128)}, u32[]{:S(2)}) copy-start(f32[16,256]{1,0:T(8,128)} %copy-done.21) | copy-start | bytes 49156
  372.5 11.9 %collective-permute-start.7 = (f32[256,64]{0,1:T(8,128)S(1)}, f32[256,64]{0,1:T(8,128)S(1)}, u32[]{:S(2)}, u32[]{:S(2)}) collective-permute-start(f32[256,64]{0,1:T(8,128)S(1)} %fusion.227), channel_id=1, source_target_pairs={{8,0},{12,4},{16,8},{20,12},{24,16},{28,20},{32,24},{36,28},{40,32... | collective-permute-start | bytes 196616 | tf_op jit(solution)/shard_map/ppermute | solution.py:12
  378.2 18.8 %collective-permute-start.6 = (f32[256,256]{1,0:T(8,128)S(1)}, f32[256,256]{1,0:T(8,128)S(1)}, u32[]{:S(2)}, u32[]{:S(2)}) collective-permute-start(f32[256,256]{1,0:T(8,128)S(1)} %pad_maximum_fusion.4), channel_id=1, source_target_pairs={{8,0},{12,4},{16,8},{20,12},{24,16},{28,20},{32,24},{36,28},{40,32... | collective-permute-start | bytes 786440 | tf_op jit(solution)/shard_map/ppermute | solution.py:12
  382.9 14.6 %collective-permute-start.5 = (f32[256,64]{0,1:T(8,128)S(1)}, f32[256,64]{0,1:T(8,128)S(1)}, u32[]{:S(2)}, u32[]{:S(2)}) collective-permute-start(f32[256,64]{0,1:T(8,128)S(1)} %fusion.242), channel_id=1, source_target_pairs={{0,8},{4,12},{8,16},{12,20},{16,24},{20,28},{24,32},{28,36},{32,40... | collective-permute-start | bytes 196616 | tf_op jit(solution)/shard_map/ppermute | solution.py:12
  384.7 12.3 %copy-start.10 = (f32[256,64]{0,1:T(8,128)}, f32[256,64]{0,1:T(8,128)S(1)}, u32[]{:S(2)}) copy-start(f32[256,64]{0,1:T(8,128)S(1)} %convolution_negate_fusion.4) | copy-start | bytes 196612
  397.8 0.6 copy-start
  447.2 0.7 copy-start.28
  473.0 0.8 copy-start.11
  474.5 22.1 %collective-permute-start.25 = (f32[16,256]{1,0:T(8,128)S(1)}, f32[16,256]{1,0:T(8,128)S(1)}, u32[]{:S(2)}, u32[]{:S(2)}) collective-permute-start(f32[16,256]{1,0:T(8,128)S(1)} %fusion.225), channel_id=1, source_target_pairs={{16,0},{20,4},{24,8},{28,12},{32,16},{36,20},{40,24},{44,28},{48,3... | collective-permute-start | bytes 49160 | tf_op jit(solution)/shard_map/ppermute | solution.py:12
  483.0 13.8 %collective-permute-start.10 = (f32[256,64]{0,1:T(8,128)S(1)}, f32[256,64]{0,1:T(8,128)S(1)}, u32[]{:S(2)}, u32[]{:S(2)}) collective-permute-start(f32[256,64]{0,1:T(8,128)S(1)} %fusion.226), channel_id=1, source_target_pairs={{16,0},{20,4},{24,8},{28,12},{32,16},{36,20},{40,24},{44,28},{48,3... | collective-permute-start | bytes 196616 | tf_op jit(solution)/shard_map/ppermute | solution.py:12
  487.9 100.0 %collective-permute-start.24 = (f32[16,256]{1,0:T(8,128)}, f32[16,256]{1,0:T(8,128)S(1)}, u32[]{:S(2)}, u32[]{:S(2)}) collective-permute-start(f32[16,256]{1,0:T(8,128)} %fusion.250), channel_id=1, source_target_pairs={{0,16},{4,20},{8,24},{12,28},{16,32},{20,36},{24,40},{28,44},{32,4... | collective-permute-start | bytes 49160 | tf_op jit(solution)/shard_map/ppermute | solution.py:12
  489.2 20.8 %collective-permute-start.9 = (f32[256,256]{1,0:T(8,128)S(1)}, f32[256,256]{1,0:T(8,128)S(1)}, u32[]{:S(2)}, u32[]{:S(2)}) collective-permute-start(f32[256,256]{1,0:T(8,128)S(1)} %pad_maximum_fusion.5), channel_id=1, source_target_pairs={{16,0},{20,4},{24,8},{28,12},{32,16},{36,20},{40,24},{44,28},{48,3... | collective-permute-start | bytes 786440 | tf_op jit(solution)/shard_map/ppermute | solution.py:12
  495.2 15.2 %collective-permute-start.8 = (f32[256,64]{0,1:T(8,128)S(1)}, f32[256,64]{0,1:T(8,128)S(1)}, u32[]{:S(2)}, u32[]{:S(2)}) collective-permute-start(f32[256,64]{0,1:T(8,128)S(1)} %fusion.243), channel_id=1, source_target_pairs={{0,16},{4,20},{8,24},{12,28},{16,32},{20,36},{24,40},{28,44},{32,4... | collective-permute-start | bytes 196616 | tf_op jit(solution)/shard_map/ppermute | solution.py:12
  497.1 0.6 copy-start.12
  510.0 0.8 copy-start.1
  586.7 0.8 copy-start.13
  588.5 17.3 %collective-permute-start.27 = (f32[16,256]{1,0:T(8,128)S(1)}, f32[16,256]{1,0:T(8,128)S(1)}, u32[]{:S(2)}, u32[]{:S(2)}) collective-permute-start(f32[16,256]{1,0:T(8,128)S(1)} %fusion.210), channel_id=1, source_target_pairs={{32,0},{36,4},{40,8},{44,12},{48,16},{52,20},{56,24},{60,28},{64,3... | collective-permute-start | bytes 49160 | tf_op jit(solution)/shard_map/ppermute | solution.py:12
  594.7 11.2 %collective-permute-start.26 = (f32[16,256]{1,0:T(8,128)S(1)}, f32[16,256]{1,0:T(8,128)S(1)}, u32[]{:S(2)}, u32[]{:S(2)}) collective-permute-start(f32[16,256]{1,0:T(8,128)S(1)} %fusion.252), channel_id=1, source_target_pairs={{0,32},{4,36},{8,40},{12,44},{16,48},{20,52},{24,56},{28,60},{32,6... | collective-permute-start | bytes 49160 | tf_op jit(solution)/shard_map/ppermute | solution.py:12
  596.4 9.5 %copy-start.24 = (f32[16,256]{1,0:T(8,128)S(1)}, f32[16,256]{1,0:T(8,128)}, u32[]{:S(2)}) copy-start(f32[16,256]{1,0:T(8,128)} %copy-done.23) | copy-start | bytes 49156
  596.4 9.7 %collective-permute-start.13 = (f32[256,64]{0,1:T(8,128)S(1)}, f32[256,64]{0,1:T(8,128)S(1)}, u32[]{:S(2)}, u32[]{:S(2)}) collective-permute-start(f32[256,64]{0,1:T(8,128)S(1)} %fusion.224), channel_id=1, source_target_pairs={{32,0},{36,4},{40,8},{44,12},{48,16},{52,20},{56,24},{60,28},{64,3... | collective-permute-start | bytes 196616 | tf_op jit(solution)/shard_map/ppermute | solution.py:12
  601.0 17.7 %collective-permute-start.12 = (f32[256,256]{1,0:T(8,128)S(1)}, f32[256,256]{1,0:T(8,128)S(1)}, u32[]{:S(2)}, u32[]{:S(2)}) collective-permute-start(f32[256,256]{1,0:T(8,128)S(1)} %pad_maximum_fusion.6), channel_id=1, source_target_pairs={{32,0},{36,4},{40,8},{44,12},{48,16},{52,20},{56,24},{60,28},{64,3... | collective-permute-start | bytes 786440 | tf_op jit(solution)/shard_map/ppermute | solution.py:12
  604.5 14.6 %collective-permute-start.11 = (f32[256,64]{0,1:T(8,128)S(1)}, f32[256,64]{0,1:T(8,128)S(1)}, u32[]{:S(2)}, u32[]{:S(2)}) collective-permute-start(f32[256,64]{0,1:T(8,128)S(1)} %fusion.244), channel_id=1, source_target_pairs={{0,32},{4,36},{8,40},{12,44},{16,48},{20,52},{24,56},{28,60},{32,6... | collective-permute-start | bytes 196616 | tf_op jit(solution)/shard_map/ppermute | solution.py:12
  606.4 12.3 %copy-start.14 = (f32[256,64]{0,1:T(8,128)}, f32[256,64]{0,1:T(8,128)S(1)}, u32[]{:S(2)}) copy-start(f32[256,64]{0,1:T(8,128)S(1)} %convolution_negate_fusion.2) | copy-start | bytes 196612
  619.5 0.6 copy-start.2
  669.0 0.7 copy-start.29
  695.0 0.8 copy-start.15
  696.5 23.1 %collective-permute-start.29 = (f32[16,256]{1,0:T(8,128)S(1)}, f32[16,256]{1,0:T(8,128)S(1)}, u32[]{:S(2)}, u32[]{:S(2)}) collective-permute-start(f32[16,256]{1,0:T(8,128)S(1)} %fusion.222), channel_id=1, source_target_pairs={{64,0},{68,4},{72,8},{76,12},{80,16},{84,20},{88,24},{92,28},{96,3... | collective-permute-start | bytes 49160 | tf_op jit(solution)/shard_map/ppermute | solution.py:12
  706.9 12.9 %collective-permute-start.16 = (f32[256,64]{0,1:T(8,128)S(1)}, f32[256,64]{0,1:T(8,128)S(1)}, u32[]{:S(2)}, u32[]{:S(2)}) collective-permute-start(f32[256,64]{0,1:T(8,128)S(1)} %fusion.223), channel_id=1, source_target_pairs={{64,0},{68,4},{72,8},{76,12},{80,16},{84,20},{88,24},{92,28},{96,3... | collective-permute-start | bytes 196616 | tf_op jit(solution)/shard_map/ppermute | solution.py:12
  711.5 100.1 %collective-permute-start.28 = (f32[16,256]{1,0:T(8,128)}, f32[16,256]{1,0:T(8,128)S(1)}, u32[]{:S(2)}, u32[]{:S(2)}) collective-permute-start(f32[16,256]{1,0:T(8,128)} %fusion.253), channel_id=1, source_target_pairs={{0,64},{4,68},{8,72},{12,76},{16,80},{20,84},{24,88},{28,92},{32,9... | collective-permute-start | bytes 49160 | tf_op jit(solution)/shard_map/ppermute | solution.py:12
  712.8 20.2 %collective-permute-start.15 = (f32[256,256]{1,0:T(8,128)S(1)}, f32[256,256]{1,0:T(8,128)S(1)}, u32[]{:S(2)}, u32[]{:S(2)}) collective-permute-start(f32[256,256]{1,0:T(8,128)S(1)} %pad_maximum_fusion.7), channel_id=1, source_target_pairs={{64,0},{68,4},{72,8},{76,12},{80,16},{84,20},{88,24},{92,28},{96,3... | collective-permute-start | bytes 786440 | tf_op jit(solution)/shard_map/ppermute | solution.py:12
  718.3 15.2 %collective-permute-start.14 = (f32[256,64]{0,1:T(8,128)S(1)}, f32[256,64]{0,1:T(8,128)S(1)}, u32[]{:S(2)}, u32[]{:S(2)}) collective-permute-start(f32[256,64]{0,1:T(8,128)S(1)} %fusion.245), channel_id=1, source_target_pairs={{0,64},{4,68},{8,72},{12,76},{16,80},{20,84},{24,88},{28,92},{32,9... | collective-permute-start | bytes 196616 | tf_op jit(solution)/shard_map/ppermute | solution.py:12
  720.1 0.6 copy-start.4
  733.0 0.8 copy-start.3
  810.4 0.8 copy-start.5
  811.9 19.1 %collective-permute-start.31 = (f32[16,256]{1,0:T(8,128)S(1)}, f32[16,256]{1,0:T(8,128)S(1)}, u32[]{:S(2)}, u32[]{:S(2)}) collective-permute-start(f32[16,256]{1,0:T(8,128)S(1)} %fusion.211), channel_id=1, source_target_pairs={{128,0},{132,4},{136,8},{140,12},{144,16},{148,20},{152,24},{156,2... | collective-permute-start | bytes 49160 | tf_op jit(solution)/shard_map/ppermute | solution.py:12
  819.5 11.5 %collective-permute-start.30 = (f32[16,256]{1,0:T(8,128)S(1)}, f32[16,256]{1,0:T(8,128)S(1)}, u32[]{:S(2)}, u32[]{:S(2)}) collective-permute-start(f32[16,256]{1,0:T(8,128)S(1)} %fusion.255), channel_id=1, source_target_pairs={{0,128},{4,132},{8,136},{12,140},{16,144},{20,148},{24,152},{28,15... | collective-permute-start | bytes 49160 | tf_op jit(solution)/shard_map/ppermute | solution.py:12
  820.8 12.3 %collective-permute-start.18 = (f32[256,256]{1,0:T(8,128)S(1)}, f32[256,256]{1,0:T(8,128)S(1)}, u32[]{:S(2)}, u32[]{:S(2)}) collective-permute-start(f32[256,256]{1,0:T(8,128)S(1)} %pad_maximum_fusion.8), channel_id=1, source_target_pairs={{128,0},{132,4},{136,8},{140,12},{144,16},{148,20},{152,24},{156,2... | collective-permute-start | bytes 786440 | tf_op jit(solution)/shard_map/ppermute | solution.py:12
  829.7 10.1 %collective-permute-start.17 = (f32[256,64]{0,1:T(8,128)S(1)}, f32[256,64]{0,1:T(8,128)S(1)}, u32[]{:S(2)}, u32[]{:S(2)}) collective-permute-start(f32[256,64]{0,1:T(8,128)S(1)} %fusion.246), channel_id=1, source_target_pairs={{0,128},{4,132},{8,136},{12,140},{16,144},{20,148},{24,152},{28,15... | collective-permute-start | bytes 196616 | tf_op jit(solution)/shard_map/ppermute | solution.py:12
  889.0 0.7 copy-start.30
  889.6 23.8 %copy-start.25 = (f32[256,16]{0,1:T(8,128)S(1)}, f32[256,16]{0,1:T(8,128)}, u32[]{:S(2)}) copy-start(f32[256,16]{0,1:T(8,128)} %subtract_bitcast_fusion) | copy-start | bytes 49156
  915.0 5.1 collective-permute-start.32
  (1 other events, 0.6 us)
where the time goes:
time: 934 us; the launch traced here: 924 us
  other arithmetic  490 us (52%)
  blocking collectives  187 us (20%)
  starting transfers between devices  114 us (12%)
  local copies, waits for them, and re-layouts  56.2 us (6%)
  matrix products  47.9 us (5%)
  between operations  13.9 us (1%)
  waiting for transfers between devices  12 us (1%)
    another operation x55, other arithmetic, invert(): lower_factor = jnp.linalg.cholesky(matrix)  276 us
    another operation x23, other arithmetic, invert(): return jax.scipy.linalg.cho_solve((lower_factor, True), identity)  158 us
    ppermute x33, starting transfers between devices, passed_along(): return lax.ppermute(shard, axis, pairs)  114 us
    all_gather x6, blocking collectives, per_device(): lax.all_gather(b_part, 'col', axis=1, tiled=True)  74 us
    all_gather x6, blocking collectives, per_device(): lax.all_gather(c_part, 'col', axis=1, tiled=True)  73.5 us
    another operation x58, local copies, waits for them, and re-layouts, invert(): return jax.scipy.linalg.cho_solve((lower_factor, True), identity)  35.5 us
    another operation x7, other arithmetic, per_device(): jnp.linalg.cholesky(b_final)  34.6 us
    dot_general x71, matrix products, matmul(): return jnp.dot(first_factor, second_factor, precision=finest)  28.7 us
  transfers between devices with their start and end apart: 33, of which 4 were waited for; matrix products, arithmetic and copies ran while one was open for 22% of the time, Pallas kernels for 0%

commit v1 on v0

--- a/solution.py
+++ b/solution.py
@@ -4,6 +4,19 @@
 from jax.sharding import PartitionSpec as P
 
 finest = lax.Precision.HIGHEST
+
+
+def gather_around(x, axis, dim):
+    ways = lax.axis_size(axis)
+    up = [(d, (d + 1) % ways) for d in range(ways)]
+    down = [(d, (d - 1) % ways) for d in range(ways)]
+    earlier, later = ([x], [x])
+    for _ in range(ways // 2):
+        earlier.append(lax.ppermute(earlier[-1], axis, up))
+    for _ in range((ways - 1) // 2):
+        later.append(lax.ppermute(later[-1], axis, down))
+    line = jnp.concatenate([*earlier[::-1], *later[1:]], axis=dim)
+    return jnp.roll(line, (lax.axis_index(axis) - ways // 2) * x.shape[dim], axis=dim)
 
 
 def passed_along(shard, axis, by):
@@ -99,7 +112,7 @@
     for level_index in range(levels):
         distance = 1 << level_index
         b_full, c_full = (
-            lax.all_gather(b_part, "col", axis=1, tiled=True),
+            gather_around(b_part, "col", 1),
             lax.all_gather(c_part, "col", axis=1, tiled=True),
         )
         inverse = invert(b_full)

time: 934 us -> 901 us (0.965)
  blocking collectives: 187 us -> 122 us
  waiting for transfers between devices: 12 us -> 47.2 us
    all_gather x6 -> x0, blocking collectives: 74 us -> none  [per_device(): lax.all_gather(b_part, 'col', axis=1, tiled=True)]
    ppermute x33, waiting for transfers between devices: 12 us -> 35.3 us  [passed_along(): return lax.ppermute(shard, axis, pairs)]
    ppermute x33, starting transfers between devices: 114 us -> 95.9 us  [passed_along(): return lax.ppermute(shard, axis, pairs)]
    ppermute x0 -> x18, starting transfers between devices: none -> 14.6 us  [the longest x6 12.3 us: gather_around(): later.append(lax.ppermute(later[-1], axis, down))]
    ppermute x0 -> x18, waiting for transfers between devices: none -> 11.9 us  [the longest x12 11.9 us: gather_around(): earlier.append(lax.ppermute(earlier[-1], axis, up))]
  transfers between devices with their start and end apart: 33 -> 51, of which waited for: 4 -> 15; matrix products, arithmetic and copies ran while one was open for 22% -> 23% of each run, Pallas kernels for 0% -> 0%
where the time goes in v1:
time: 901 us; the launch traced here: 885 us
  other arithmetic  493 us (55%)
  blocking collectives  122 us (14%)
  starting transfers between devices  110 us (12%)
  local copies, waits for them, and re-layouts  49.3 us (5%)
  waiting for transfers between devices  47.2 us (5%)
  matrix products  46.5 us (5%)
  between operations  13.8 us (2%)
    another operation x55, other arithmetic, invert(): lower_factor = jnp.linalg.cholesky(matrix)  276 us
    another operation x23, other arithmetic, invert(): return jax.scipy.linalg.cho_solve((lower_factor, True), identity)  158 us
    ppermute x33, starting transfers between devices, passed_along(): return lax.ppermute(shard, axis, pairs)  95.9 us
    all_gather x6, blocking collectives, per_device(): lax.all_gather(c_part, 'col', axis=1, tiled=True)  82.7 us
    ppermute x33, waiting for transfers between devices, passed_along(): return lax.ppermute(shard, axis, pairs)  35.3 us
    another operation x58, local copies, waits for them, and re-layouts, invert(): return jax.scipy.linalg.cho_solve((lower_factor, True), identity)  35 us
    another operation x7, other arithmetic, per_device(): jnp.linalg.cholesky(b_final)  34.7 us
    dot_general x71, matrix products, matmul(): return jnp.dot(first_factor, second_factor, precision=finest)  27.2 us
  transfers between devices with their start and end apart: 51, of which 15 were waited for; matrix products, arithmetic and copies ran while one was open for 23% of the time, Pallas kernels for 0%

profile of v1, /device:TPU:250, one launch (start us, length us, event | category | flops | bytes accessed | tf_op | source)
XLA Modules:
  0.0 885.5 jit_solution(9501200632800768447)
XLA Ops:
  1.0 13.5 %all_gather.27 = f32[2,256,256]{2,0,1:T(2,128)S(1)} all-gather(f32[2,64,256]{2,0,1:T(2,128)S(1)} %copy.26), channel_id=1, replica_groups=mesh['chain'=64,'col'=4] {'col'}, dimensions={1}, use_global_device_ids=true | all-gather | bytes 655360 | tf_op jit(solution)/shard_map/all_gather | solution.py:66
  15.1 11.7 %cholesky.424 = f32[128,128]{1,0:T(8,128)S(1)} custom-call(f32[128,128]{1,0:T(8,128)S(1)} %cholesky.726), custom_call_target="Cholesky" | custom-call | tf_op jit(solution)/shard_map/jit(cholesky)/cholesky | solution.py:33
  26.9 9.8 %custom-call.36 = f32[1,128,128]{1,2,0:T(8,128)S(1)} custom-call(f32[1,128,128]{2,1,0:T(8,128)S(1)} %get-tuple-element.385), custom_call_target="InvertDiagBlocksLowerTriangular" | custom-call | tf_op jit(solution)/shard_map/jit(cholesky)/cholesky | solution.py:33
  37.2 11.7 %cholesky.441 = f32[128,128]{1,0:T(8,128)S(1)} custom-call(f32[128,128]{1,0:T(8,128)S(1)} %convolution_subtract_fusion.24), custom_call_target="Cholesky" | custom-call | tf_op jit(solution)/shard_map/jit(cholesky)/cholesky | solution.py:33
  51.0 4.5 while.67
  55.5 19.7 %custom-call.37 = f32[2,128,128]{1,2,0:T(8,128)S(1)} custom-call(f32[2,128,128]{2,1,0:T(8,128)S(1)} %get-tuple-element.219), custom_call_target="InvertDiagBlocksLowerTriangular" | custom-call | tf_op jit(solution)/shard_map/jit(_cho_solve)/triangular_solve | solution.py:35
  77.6 14.0 %all_gather.28 = f32[3,256,256]{2,1,0:T(8,128)S(1)} all-gather(f32[3,64,256]{2,1,0:T(8,128)S(1)} %copy-done.13), channel_id=1, replica_groups=mesh['chain'=64,'col'=4] {'col'}, dimensions={1}, use_global_device_ids=true | all-gather | bytes 983040 | tf_op jit(solution)/shard_map/all_gather | solution.py:67
  93.7 11.7 %cholesky.458 = f32[128,128]{1,0:T(8,128)S(1)} custom-call(f32[128,128]{1,0:T(8,128)S(1)} %cholesky.729), custom_call_target="Cholesky" | custom-call | tf_op jit(solution)/shard_map/while/body/eval_jaxpr/jit(cholesky)/cholesky | solution.py:33
  105.5 9.8 %custom-call.38 = f32[1,128,128]{1,2,0:T(8,128)S(1)} custom-call(f32[1,128,128]{2,1,0:T(8,128)S(1)} %get-tuple-element.381), custom_call_target="InvertDiagBlocksLowerTriangular" | custom-call | tf_op jit(solution)/shard_map/while/body/eval_jaxpr/jit(cholesky)/cholesky | solution.py:33
  115.8 11.7 %cholesky.475 = f32[128,128]{1,0:T(8,128)S(1)} custom-call(f32[128,128]{1,0:T(8,128)S(1)} %convolution_subtract_fusion.23), custom_call_target="Cholesky" | custom-call | tf_op jit(solution)/shard_map/while/body/eval_jaxpr/jit(cholesky)/cholesky | solution.py:33
  134.3 19.7 %custom-call.39 = f32[2,128,128]{1,2,0:T(8,128)S(1)} custom-call(f32[2,128,128]{2,1,0:T(8,128)S(1)} %get-tuple-element.220), custom_call_target="InvertDiagBlocksLowerTriangular" | custom-call | tf_op jit(solution)/shard_map/while/body/eval_jaxpr/jit(_cho_solve)/triangular_solve | solution.py:35
  174.8 13.4 %all_gather.29 = f32[256,256]{0,1:T(8,128)S(1)} all-gather(f32[256,64]{0,1:T(8,128)S(1)} %bitcast.554), channel_id=1, replica_groups=mesh['chain'=64,'col'=4] {'col'}, dimensions={1}, use_global_device_ids=true | all-gather | bytes 327680 | tf_op jit(solution)/shard_map/all_gather | solution.py:116
  188.8 11.7 %cholesky.492 = f32[128,128]{1,0:T(8,128)S(1)} custom-call(f32[128,128]{1,0:T(8,128)S(1)} %cholesky.732), custom_call_target="Cholesky" | custom-call | tf_op jit(solution)/shard_map/jit(cholesky)/cholesky | solution.py:33
  200.6 9.8 %custom-call.40 = f32[1,128,128]{1,2,0:T(8,128)S(1)} custom-call(f32[1,128,128]{2,1,0:T(8,128)S(1)} %get-tuple-element.377), custom_call_target="InvertDiagBlocksLowerTriangular" | custom-call | tf_op jit(solution)/shard_map/jit(cholesky)/cholesky | solution.py:33
  210.9 11.7 %cholesky.509 = f32[128,128]{1,0:T(8,128)S(1)} custom-call(f32[128,128]{1,0:T(8,128)S(1)} %convolution_subtract_fusion.22), custom_call_target="Cholesky" | custom-call | tf_op jit(solution)/shard_map/jit(cholesky)/cholesky | solution.py:33
  225.9 4.3 while.69
  230.2 19.7 %custom-call.41 = f32[2,128,128]{1,2,0:T(8,128)S(1)} custom-call(f32[2,128,128]{2,1,0:T(8,128)S(1)} %get-tuple-element.221), custom_call_target="InvertDiagBlocksLowerTriangular" | custom-call | tf_op jit(solution)/shard_map/jit(_cho_solve)/triangular_solve | solution.py:35
  273.6 13.7 %all_gather.30 = f32[256,256]{0,1:T(8,128)S(1)} all-gather(f32[256,64]{0,1:T(8,128)S(1)} %convolution_negate_fusion.5), channel_id=1, replica_groups=mesh['chain'=64,'col'=4] {'col'}, dimensions={1}, use_global_device_ids=true | all-gather | bytes 327680 | tf_op jit(solution)/shard_map/all_gather | solution.py:116
  287.9 11.7 %cholesky.526 = f32[128,128]{1,0:T(8,128)S(1)} custom-call(f32[128,128]{1,0:T(8,128)S(1)} %cholesky.735), custom_call_target="Cholesky" | custom-call | tf_op jit(solution)/shard_map/jit(cholesky)/cholesky | solution.py:33
  299.7 9.8 %custom-call.42 = f32[1,128,128]{1,2,0:T(8,128)S(1)} custom-call(f32[1,128,128]{2,1,0:T(8,128)S(1)} %get-tuple-element.373), custom_call_target="InvertDiagBlocksLowerTriangular" | custom-call | tf_op jit(solution)/shard_map/jit(cholesky)/cholesky | solution.py:33
  310.0 11.7 %cholesky.543 = f32[128,128]{1,0:T(8,128)S(1)} custom-call(f32[128,128]{1,0:T(8,128)S(1)} %convolution_subtract_fusion.21), custom_call_target="Cholesky" | custom-call | tf_op jit(solution)/shard_map/jit(cholesky)/cholesky | solution.py:33
  324.4 5.4 while.70
  329.8 19.7 %custom-call.43 = f32[2,128,128]{1,2,0:T(8,128)S(1)} custom-call(f32[2,128,128]{2,1,0:T(8,128)S(1)} %get-tuple-element.222), custom_call_target="InvertDiagBlocksLowerTriangular" | custom-call | tf_op jit(solution)/shard_map/jit(_cho_solve)/triangular_solve | solution.py:35
  358.3 4.7 collective-permute-start.12
  363.4 5.5 collective-permute-start.13
  380.0 13.8 %all_gather.31 = f32[256,256]{0,1:T(8,128)S(1)} all-gather(f32[256,64]{0,1:T(8,128)S(1)} %convolution_negate_fusion.4), channel_id=1, replica_groups=mesh['chain'=64,'col'=4] {'col'}, dimensions={1}, use_global_device_ids=true | all-gather | bytes 327680 | tf_op jit(solution)/shard_map/all_gather | solution.py:116
  394.5 11.7 %cholesky.560 = f32[128,128]{1,0:T(8,128)S(1)} custom-call(f32[128,128]{1,0:T(8,128)S(1)} %cholesky.738), custom_call_target="Cholesky" | custom-call | tf_op jit(solution)/shard_map/jit(cholesky)/cholesky | solution.py:33
  406.3 9.8 %custom-call.44 = f32[1,128,128]{1,2,0:T(8,128)S(1)} custom-call(f32[1,128,128]{2,1,0:T(8,128)S(1)} %get-tuple-element.369), custom_call_target="InvertDiagBlocksLowerTriangular" | custom-call | tf_op jit(solution)/shard_map/jit(cholesky)/cholesky | solution.py:33
  416.6 11.7 %cholesky.577 = f32[128,128]{1,0:T(8,128)S(1)} custom-call(f32[128,128]{1,0:T(8,128)S(1)} %convolution_subtract_fusion.20), custom_call_target="Cholesky" | custom-call | tf_op jit(solution)/shard_map/jit(cholesky)/cholesky | solution.py:33
  435.5 19.7 %custom-call.45 = f32[2,128,128]{1,2,0:T(8,128)S(1)} custom-call(f32[2,128,128]{2,1,0:T(8,128)S(1)} %get-tuple-element.223), custom_call_target="InvertDiagBlocksLowerTriangular" | custom-call | tf_op jit(solution)/shard_map/jit(_cho_solve)/triangular_solve | solution.py:35
  457.6 6.1 collective-permute-start.43
  467.6 5.3 collective-permute-start.19
  476.3 6.3 collective-permute-done.17
  487.5 14.0 %all_gather.32 = f32[256,256]{0,1:T(8,128)S(1)} all-gather(f32[256,64]{0,1:T(8,128)S(1)} %convolution_negate_fusion.3), channel_id=1, replica_groups=mesh['chain'=64,'col'=4] {'col'}, dimensions={1}, use_global_device_ids=true | all-gather | bytes 327680 | tf_op jit(solution)/shard_map/all_gather | solution.py:116
  502.2 11.7 %cholesky.594 = f32[128,128]{1,0:T(8,128)S(1)} custom-call(f32[128,128]{1,0:T(8,128)S(1)} %cholesky.741), custom_call_target="Cholesky" | custom-call | tf_op jit(solution)/shard_map/jit(cholesky)/cholesky | solution.py:33
  514.0 9.8 %custom-call.46 = f32[1,128,128]{1,2,0:T(8,128)S(1)} custom-call(f32[1,128,128]{2,1,0:T(8,128)S(1)} %get-tuple-element.365), custom_call_target="InvertDiagBlocksLowerTriangular" | custom-call | tf_op jit(solution)/shard_map/jit(cholesky)/cholesky | solution.py:33
  524.3 11.7 %cholesky.611 = f32[128,128]{1,0:T(8,128)S(1)} custom-call(f32[128,128]{1,0:T(8,128)S(1)} %convolution_subtract_fusion.19), custom_call_target="Cholesky" | custom-call | tf_op jit(solution)/shard_map/jit(cholesky)/cholesky | solution.py:33
  538.7 5.6 while.72
  544.3 19.7 %custom-call.47 = f32[2,128,128]{1,2,0:T(8,128)S(1)} custom-call(f32[2,128,128]{2,1,0:T(8,128)S(1)} %get-tuple-element.224), custom_call_target="InvertDiagBlocksLowerTriangular" | custom-call | tf_op jit(solution)/shard_map/jit(_cho_solve)/triangular_solve | solution.py:35
  567.4 4.6 collective-permute-start.45
  573.6 4.6 collective-permute-start.24
  584.4 4.1 collective-permute-done.23
  593.5 13.9 %all_gather.33 = f32[256,256]{0,1:T(8,128)S(1)} all-gather(f32[256,64]{0,1:T(8,128)S(1)} %convolution_negate_fusion.2), channel_id=1, replica_groups=mesh['chain'=64,'col'=4] {'col'}, dimensions={1}, use_global_device_ids=true | all-gather | bytes 327680 | tf_op jit(solution)/shard_map/all_gather | solution.py:116
  608.1 11.7 %cholesky.628 = f32[128,128]{1,0:T(8,128)S(1)} custom-call(f32[128,128]{1,0:T(8,128)S(1)} %cholesky.744), custom_call_target="Cholesky" | custom-call | tf_op jit(solution)/shard_map/jit(cholesky)/cholesky | solution.py:33
  619.8 9.8 %custom-call.48 = f32[1,128,128]{1,2,0:T(8,128)S(1)} custom-call(f32[1,128,128]{2,1,0:T(8,128)S(1)} %get-tuple-element.361), custom_call_target="InvertDiagBlocksLowerTriangular" | custom-call | tf_op jit(solution)/shard_map/jit(cholesky)/cholesky | solution.py:33
  630.1 11.7 %cholesky.645 = f32[128,128]{1,0:T(8,128)S(1)} custom-call(f32[128,128]{1,0:T(8,128)S(1)} %convolution_subtract_fusion.18), custom_call_target="Cholesky" | custom-call | tf_op jit(solution)/shard_map/jit(cholesky)/cholesky | solution.py:33
  649.1 19.7 %custom-call.49 = f32[2,128,128]{1,2,0:T(8,128)S(1)} custom-call(f32[2,128,128]{2,1,0:T(8,128)S(1)} %get-tuple-element.225), custom_call_target="InvertDiagBlocksLowerTriangular" | custom-call | tf_op jit(solution)/shard_map/jit(_cho_solve)/triangular_solve | solution.py:35
  671.3 4.6 collective-permute-start.47
  684.7 6.4 collective-permute-done.29
  696.1 13.9 %all_gather.34 = f32[256,256]{0,1:T(8,128)S(1)} all-gather(f32[256,64]{0,1:T(8,128)S(1)} %convolution_negate_fusion.1), channel_id=1, replica_groups=mesh['chain'=64,'col'=4] {'col'}, dimensions={1}, use_global_device_ids=true | all-gather | bytes 327680 | tf_op jit(solution)/shard_map/all_gather | solution.py:116
  710.6 11.7 %cholesky.662 = f32[128,128]{1,0:T(8,128)S(1)} custom-call(f32[128,128]{1,0:T(8,128)S(1)} %cholesky.747), custom_call_target="Cholesky" | custom-call | tf_op jit(solution)/shard_map/jit(cholesky)/cholesky | solution.py:33
  722.4 9.8 %custom-call.50 = f32[1,128,128]{1,2,0:T(8,128)S(1)} custom-call(f32[1,128,128]{2,1,0:T(8,128)S(1)} %get-tuple-element.357), custom_call_target="InvertDiagBlocksLowerTriangular" | custom-call | tf_op jit(solution)/shard_map/jit(cholesky)/cholesky | solution.py:33
  732.7 11.7 %cholesky.679 = f32[128,128]{1,0:T(8,128)S(1)} custom-call(f32[128,128]{1,0:T(8,128)S(1)} %convolution_subtract_fusion.17), custom_call_target="Cholesky" | custom-call | tf_op jit(solution)/shard_map/jit(cholesky)/cholesky | solution.py:33
  747.1 5.4 while.74
  752.5 19.7 %custom-call.51 = f32[2,128,128]{1,2,0:T(8,128)S(1)} custom-call(f32[2,128,128]{2,1,0:T(8,128)S(1)} %get-tuple-element.226), custom_call_target="InvertDiagBlocksLowerTriangular" | custom-call | tf_op jit(solution)/shard_map/jit(_cho_solve)/triangular_solve | solution.py:35
  775.2 5.6 collective-permute-start.49
  782.4 8.5 collective-permute-start.36
  795.2 6.3 collective-permute-done.35
  801.9 12.3 %all_gather.35 = f32[256,256]{0,1:T(8,128)S(1)} all-gather(f32[256,64]{0,1:T(8,128)S(1)} %subtract_subtract_fusion), channel_id=1, replica_groups=mesh['chain'=64,'col'=4] {'col'}, dimensions={1}, use_global_device_ids=true | all-gather | bytes 327680 | tf_op jit(solution)/shard_map/all_gather | solution.py:131
  814.4 11.7 %cholesky.696 = f32[128,128]{1,0:T(8,128)S(1)} custom-call(f32[128,128]{1,0:T(8,128)S(1)} %cholesky.750), custom_call_target="Cholesky" | custom-call | tf_op jit(solution)/shard_map/jit(cholesky)/cholesky | solution.py:132
  826.1 9.8 %custom-call.52 = f32[1,128,128]{1,2,0:T(8,128)S(1)} custom-call(f32[1,128,128]{2,1,0:T(8,128)S(1)} %get-tuple-element.353), custom_call_target="InvertDiagBlocksLowerTriangular" | custom-call | tf_op jit(solution)/shard_map/jit(cholesky)/cholesky | solution.py:132
  836.4 11.7 %cholesky.713 = f32[128,128]{1,0:T(8,128)S(1)} custom-call(f32[128,128]{1,0:T(8,128)S(1)} %convolution_subtract_fusion.16), custom_call_target="Cholesky" | custom-call | tf_op jit(solution)/shard_map/jit(cholesky)/cholesky | solution.py:132
  851.5 4.2 while.66
  855.7 19.7 %custom-call.20 = f32[2,128,128]{1,2,0:T(8,128)S(1)} custom-call(f32[2,128,128]{2,1,0:T(8,128)S(1)} %get-tuple-element.176), custom_call_target="InvertDiagBlocksLowerTriangular" | custom-call | tf_op jit(solution)/shard_map/jit(_cho_solve)/triangular_solve | solution.py:132
  (464 shorter events, 212.2 us)
Async XLA Ops:
  134.3 20.0 %copy-start.20 = (s32[2,2]{1,0:T(2,128)}, s32[2,2]{1,0:T(2,128)S(1)}, u32[]{:S(2)}) copy-start(s32[2,2]{1,0:T(2,128)S(1)} %get-tuple-element.1037) | copy-start | bytes 52
  158.1 9.5 %collective-permute-start.37 = (f32[16,256]{1,0:T(8,128)S(1)}, f32[16,256]{1,0:T(8,128)S(1)}, u32[]{:S(2)}, u32[]{:S(2)}) collective-permute-start(f32[16,256]{1,0:T(8,128)S(1)} %convolution_subtract_fusion.29), channel_id=1, source_target_pairs={{4,0},{8,4},{12,8},{16,12},{20,16},{24,20},{28,24},{32,28},{36,32}... | collective-permute-start | bytes 49160 | tf_op jit(solution)/shard_map/ppermute | solution.py:25
  161.6 6.9 collective-permute-start
  165.2 5.0 collective-permute-start.1
  170.1 18.0 %copy-start.6 = (f32[256,64]{0,1:T(8,128)}, f32[256,64]{0,1:T(8,128)S(1)}, u32[]{:S(2)}) copy-start(f32[256,64]{0,1:T(8,128)S(1)} %fusion.17) | copy-start | bytes 196612
  170.2 4.3 collective-permute-start.2
  170.6 17.5 %collective-permute-start.4 = (f32[256,64]{0,1:T(8,128)S(1)}, f32[256,64]{0,1:T(8,128)S(1)}, u32[]{:S(2)}, u32[]{:S(2)}) collective-permute-start(f32[256,64]{0,1:T(8,128)S(1)} %fusion.17), channel_id=1, source_target_pairs={{0,3},{1,0},{2,1},{3,2},{4,7},{5,4},{6,5},{7,6},{8,11},{9,8},{10,9... | collective-permute-start | bytes 196616 | tf_op jit(solution)/shard_map/ppermute | solution.py:17
  174.5 13.7 %collective-permute-start.3 = (f32[256,64]{0,1:T(8,128)S(1)}, f32[256,64]{0,1:T(8,128)S(1)}, u32[]{:S(2)}, u32[]{:S(2)}) collective-permute-start(f32[256,64]{0,1:T(8,128)S(1)} %collective-permute-done.2), channel_id=1, source_target_pairs={{0,1},{1,2},{2,3},{3,0},{4,5},{5,6},{6,7},{7,4},{8,9},{9,10},{10,1... | collective-permute-start | bytes 196616 | tf_op jit(solution)/shard_map/ppermute | solution.py:15
  252.3 12.0 %collective-permute-start.39 = (f32[16,256]{1,0:T(8,128)S(1)}, f32[16,256]{1,0:T(8,128)S(1)}, u32[]{:S(2)}, u32[]{:S(2)}) collective-permute-start(f32[16,256]{1,0:T(8,128)S(1)} %fusion.268), channel_id=1, source_target_pairs={{4,0},{8,4},{12,8},{16,12},{20,16},{24,20},{28,24},{32,28},{36,32}... | collective-permute-start | bytes 49160 | tf_op jit(solution)/shard_map/ppermute | solution.py:25
  254.3 10.3 %collective-permute-start.6 = (f32[256,256]{1,0:T(8,128)S(1)}, f32[256,256]{1,0:T(8,128)S(1)}, u32[]{:S(2)}, u32[]{:S(2)}) collective-permute-start(f32[256,256]{1,0:T(8,128)S(1)} %pad_maximum_fusion.3), channel_id=1, source_target_pairs={{4,0},{8,4},{12,8},{16,12},{20,16},{24,20},{28,24},{32,28},{36,32}... | collective-permute-start | bytes 786440 | tf_op jit(solution)/shard_map/ppermute | solution.py:25
  258.1 10.6 %collective-permute-start.7 = (f32[256,64]{0,1:T(8,128)S(1)}, f32[256,64]{0,1:T(8,128)S(1)}, u32[]{:S(2)}, u32[]{:S(2)}) collective-permute-start(f32[256,64]{0,1:T(8,128)S(1)} %fusion.269), channel_id=1, source_target_pairs={{4,0},{8,4},{12,8},{16,12},{20,16},{24,20},{28,24},{32,28},{36,32}... | collective-permute-start | bytes 196616 | tf_op jit(solution)/shard_map/ppermute | solution.py:25
  260.0 92.2 %collective-permute-start.38 = (f32[16,256]{1,0:T(8,128)}, f32[16,256]{1,0:T(8,128)S(1)}, u32[]{:S(2)}, u32[]{:S(2)}) collective-permute-start(f32[16,256]{1,0:T(8,128)} %fusion.287), channel_id=1, source_target_pairs={{0,4},{4,8},{8,12},{12,16},{16,20},{20,24},{24,28},{28,32},{32,36}... | collective-permute-start | bytes 49160 | tf_op jit(solution)/shard_map/ppermute | solution.py:25
  262.4 5.6 collective-permute-start.5
  264.6 3.4 copy-start.7
  268.4 5.0 collective-permute-start.8
  269.0 18.3 %copy-start.8 = (f32[256,64]{0,1:T(8,128)}, f32[256,64]{0,1:T(8,128)S(1)}, u32[]{:S(2)}) copy-start(f32[256,64]{0,1:T(8,128)S(1)} %convolution_negate_fusion.5) | copy-start | bytes 196612
  269.0 18.3 %collective-permute-start.10 = (f32[256,64]{0,1:T(8,128)S(1)}, f32[256,64]{0,1:T(8,128)S(1)}, u32[]{:S(2)}, u32[]{:S(2)}) collective-permute-start(f32[256,64]{0,1:T(8,128)S(1)} %subtract_subtract_fusion.5), channel_id=1, source_target_pairs={{0,3},{1,0},{2,1},{3,2},{4,7},{5,4},{6,5},{7,6},{8,11},{9,8},{10,9... | collective-permute-start | bytes 196616 | tf_op jit(solution)/shard_map/ppermute | solution.py:17
  273.4 13.9 %collective-permute-start.9 = (f32[256,64]{0,1:T(8,128)S(1)}, f32[256,64]{0,1:T(8,128)S(1)}, u32[]{:S(2)}, u32[]{:S(2)}) collective-permute-start(f32[256,64]{0,1:T(8,128)S(1)} %collective-permute-done.8), channel_id=1, source_target_pairs={{0,1},{1,2},{2,3},{3,0},{4,5},{5,6},{6,7},{7,4},{8,9},{9,10},{10,1... | collective-permute-start | bytes 196616 | tf_op jit(solution)/shard_map/ppermute | solution.py:15
  352.9 17.3 %collective-permute-start.41 = (f32[16,256]{1,0:T(8,128)S(1)}, f32[16,256]{1,0:T(8,128)S(1)}, u32[]{:S(2)}, u32[]{:S(2)}) collective-permute-start(f32[16,256]{1,0:T(8,128)S(1)} %fusion.249), channel_id=1, source_target_pairs={{8,0},{12,4},{16,8},{20,12},{24,16},{28,20},{32,24},{36,28},{40,32... | collective-permute-start | bytes 49160 | tf_op jit(solution)/shard_map/ppermute | solution.py:25
  357.0 13.2 %copy-start.16 = (f32[16,256]{1,0:T(8,128)S(1)}, f32[16,256]{1,0:T(8,128)}, u32[]{:S(2)}) copy-start(f32[16,256]{1,0:T(8,128)} %copy-done.15) | copy-start | bytes 49156
  357.0 13.1 %collective-permute-start.40 = (f32[16,256]{1,0:T(8,128)S(1)}, f32[16,256]{1,0:T(8,128)S(1)}, u32[]{:S(2)}, u32[]{:S(2)}) collective-permute-start(f32[16,256]{1,0:T(8,128)S(1)} %fusion.289), channel_id=1, source_target_pairs={{0,8},{4,12},{8,16},{12,20},{16,24},{20,28},{24,32},{28,36},{32,40... | collective-permute-start | bytes 49160 | tf_op jit(solution)/shard_map/ppermute | solution.py:25
  358.3 12.1 %collective-permute-start.12 = (f32[256,256]{1,0:T(8,128)S(1)}, f32[256,256]{1,0:T(8,128)S(1)}, u32[]{:S(2)}, u32[]{:S(2)}) collective-permute-start(f32[256,256]{1,0:T(8,128)S(1)} %pad_maximum_fusion.4), channel_id=1, source_target_pairs={{8,0},{12,4},{16,8},{20,12},{24,16},{28,20},{32,24},{36,28},{40,32... | collective-permute-start | bytes 786440 | tf_op jit(solution)/shard_map/ppermute | solution.py:25
  363.4 12.1 %collective-permute-start.13 = (f32[256,64]{0,1:T(8,128)S(1)}, f32[256,64]{0,1:T(8,128)S(1)}, u32[]{:S(2)}, u32[]{:S(2)}) collective-permute-start(f32[256,64]{0,1:T(8,128)S(1)} %fusion.267), channel_id=1, source_target_pairs={{8,0},{12,4},{16,8},{20,12},{24,16},{28,20},{32,24},{36,28},{40,32... | collective-permute-start | bytes 196616 | tf_op jit(solution)/shard_map/ppermute | solution.py:25
  368.8 6.2 collective-permute-start.11
  375.4 18.5 %copy-start = (f32[256,64]{0,1:T(8,128)}, f32[256,64]{0,1:T(8,128)S(1)}, u32[]{:S(2)}) copy-start(f32[256,64]{0,1:T(8,128)S(1)} %subtract_subtract_fusion.4) | copy-start | bytes 196612
  375.4 4.3 collective-permute-start.14
  375.8 18.1 %collective-permute-start.16 = (f32[256,64]{0,1:T(8,128)S(1)}, f32[256,64]{0,1:T(8,128)S(1)}, u32[]{:S(2)}, u32[]{:S(2)}) collective-permute-start(f32[256,64]{0,1:T(8,128)S(1)} %subtract_subtract_fusion.4), channel_id=1, source_target_pairs={{0,3},{1,0},{2,1},{3,2},{4,7},{5,4},{6,5},{7,6},{8,11},{9,8},{10,9... | collective-permute-start | bytes 196616 | tf_op jit(solution)/shard_map/ppermute | solution.py:17
  379.7 14.1 %collective-permute-start.15 = (f32[256,64]{0,1:T(8,128)S(1)}, f32[256,64]{0,1:T(8,128)S(1)}, u32[]{:S(2)}, u32[]{:S(2)}) collective-permute-start(f32[256,64]{0,1:T(8,128)S(1)} %collective-permute-done.14), channel_id=1, source_target_pairs={{0,1},{1,2},{2,3},{3,0},{4,5},{5,6},{6,7},{7,4},{8,9},{9,10},{10,1... | collective-permute-start | bytes 196616 | tf_op jit(solution)/shard_map/ppermute | solution.py:15
  457.6 17.9 %collective-permute-start.43 = (f32[16,256]{1,0:T(8,128)S(1)}, f32[16,256]{1,0:T(8,128)S(1)}, u32[]{:S(2)}, u32[]{:S(2)}) collective-permute-start(f32[16,256]{1,0:T(8,128)S(1)} %fusion.265), channel_id=1, source_target_pairs={{16,0},{20,4},{24,8},{28,12},{32,16},{36,20},{40,24},{44,28},{48,3... | collective-permute-start | bytes 49160 | tf_op jit(solution)/shard_map/ppermute | solution.py:25
  463.8 12.0 %collective-permute-start.18 = (f32[256,256]{1,0:T(8,128)S(1)}, f32[256,256]{1,0:T(8,128)S(1)}, u32[]{:S(2)}, u32[]{:S(2)}) collective-permute-start(f32[256,256]{1,0:T(8,128)S(1)} %pad_maximum_fusion.5), channel_id=1, source_target_pairs={{16,0},{20,4},{24,8},{28,12},{32,16},{36,20},{40,24},{44,28},{48,3... | collective-permute-start | bytes 786440 | tf_op jit(solution)/shard_map/ppermute | solution.py:25
  467.6 15.4 %collective-permute-start.19 = (f32[256,64]{0,1:T(8,128)S(1)}, f32[256,64]{0,1:T(8,128)S(1)}, u32[]{:S(2)}, u32[]{:S(2)}) collective-permute-start(f32[256,64]{0,1:T(8,128)S(1)} %fusion.266), channel_id=1, source_target_pairs={{16,0},{20,4},{24,8},{28,12},{32,16},{36,20},{40,24},{44,28},{48,3... | collective-permute-start | bytes 196616 | tf_op jit(solution)/shard_map/ppermute | solution.py:25
  472.9 93.8 %collective-permute-start.42 = (f32[16,256]{1,0:T(8,128)}, f32[16,256]{1,0:T(8,128)S(1)}, u32[]{:S(2)}, u32[]{:S(2)}) collective-permute-start(f32[16,256]{1,0:T(8,128)} %fusion.290), channel_id=1, source_target_pairs={{0,16},{4,20},{8,24},{12,28},{16,32},{20,36},{24,40},{28,44},{32,4... | collective-permute-start | bytes 49160 | tf_op jit(solution)/shard_map/ppermute | solution.py:25
  474.2 8.3 collective-permute-start.17
  475.8 6.8 copy-start.1
  482.9 4.3 collective-permute-start.20
  483.3 18.3 %copy-start.10 = (f32[256,64]{0,1:T(8,128)}, f32[256,64]{0,1:T(8,128)S(1)}, u32[]{:S(2)}) copy-start(f32[256,64]{0,1:T(8,128)S(1)} %convolution_negate_fusion.3) | copy-start | bytes 196612
  483.3 18.3 %collective-permute-start.22 = (f32[256,64]{0,1:T(8,128)S(1)}, f32[256,64]{0,1:T(8,128)S(1)}, u32[]{:S(2)}, u32[]{:S(2)}) collective-permute-start(f32[256,64]{0,1:T(8,128)S(1)} %subtract_subtract_fusion.3), channel_id=1, source_target_pairs={{0,3},{1,0},{2,1},{3,2},{4,7},{5,4},{6,5},{7,6},{8,11},{9,8},{10,9... | collective-permute-start | bytes 196616 | tf_op jit(solution)/shard_map/ppermute | solution.py:17
  487.3 14.3 %collective-permute-start.21 = (f32[256,64]{0,1:T(8,128)S(1)}, f32[256,64]{0,1:T(8,128)S(1)}, u32[]{:S(2)}, u32[]{:S(2)}) collective-permute-start(f32[256,64]{0,1:T(8,128)S(1)} %collective-permute-done.20), channel_id=1, source_target_pairs={{0,1},{1,2},{2,3},{3,0},{4,5},{5,6},{6,7},{7,4},{8,9},{9,10},{10,1... | collective-permute-start | bytes 196616 | tf_op jit(solution)/shard_map/ppermute | solution.py:15
  567.4 16.3 %collective-permute-start.45 = (f32[16,256]{1,0:T(8,128)S(1)}, f32[16,256]{1,0:T(8,128)S(1)}, u32[]{:S(2)}, u32[]{:S(2)}) collective-permute-start(f32[16,256]{1,0:T(8,128)S(1)} %fusion.250), channel_id=1, source_target_pairs={{32,0},{36,4},{40,8},{44,12},{48,16},{52,20},{56,24},{60,28},{64,3... | collective-permute-start | bytes 49160 | tf_op jit(solution)/shard_map/ppermute | solution.py:25
  572.2 11.5 %copy-start.18 = (f32[16,256]{1,0:T(8,128)S(1)}, f32[16,256]{1,0:T(8,128)}, u32[]{:S(2)}) copy-start(f32[16,256]{1,0:T(8,128)} %copy-done.17) | copy-start | bytes 49156
  572.3 11.4 %collective-permute-start.44 = (f32[16,256]{1,0:T(8,128)S(1)}, f32[16,256]{1,0:T(8,128)S(1)}, u32[]{:S(2)}, u32[]{:S(2)}) collective-permute-start(f32[16,256]{1,0:T(8,128)S(1)} %fusion.292), channel_id=1, source_target_pairs={{0,32},{4,36},{8,40},{12,44},{16,48},{20,52},{24,56},{28,60},{32,6... | collective-permute-start | bytes 49160 | tf_op jit(solution)/shard_map/ppermute | solution.py:25
  573.6 10.3 %collective-permute-start.24 = (f32[256,256]{1,0:T(8,128)S(1)}, f32[256,256]{1,0:T(8,128)S(1)}, u32[]{:S(2)}, u32[]{:S(2)}) collective-permute-start(f32[256,256]{1,0:T(8,128)S(1)} %pad_maximum_fusion.6), channel_id=1, source_target_pairs={{32,0},{36,4},{40,8},{44,12},{48,16},{52,20},{56,24},{60,28},{64,3... | collective-permute-start | bytes 786440 | tf_op jit(solution)/shard_map/ppermute | solution.py:25
  578.5 10.5 %collective-permute-start.25 = (f32[256,64]{0,1:T(8,128)S(1)}, f32[256,64]{0,1:T(8,128)S(1)}, u32[]{:S(2)}, u32[]{:S(2)}) collective-permute-start(f32[256,64]{0,1:T(8,128)S(1)} %fusion.264), channel_id=1, source_target_pairs={{32,0},{36,4},{40,8},{44,12},{48,16},{52,20},{56,24},{60,28},{64,3... | collective-permute-start | bytes 196616 | tf_op jit(solution)/shard_map/ppermute | solution.py:25
  582.4 6.2 collective-permute-start.23
  588.9 18.5 %copy-start.2 = (f32[256,64]{0,1:T(8,128)}, f32[256,64]{0,1:T(8,128)S(1)}, u32[]{:S(2)}) copy-start(f32[256,64]{0,1:T(8,128)S(1)} %subtract_subtract_fusion.2) | copy-start | bytes 196612
  588.9 4.3 collective-permute-start.26
  589.3 18.1 %collective-permute-start.28 = (f32[256,64]{0,1:T(8,128)S(1)}, f32[256,64]{0,1:T(8,128)S(1)}, u32[]{:S(2)}, u32[]{:S(2)}) collective-permute-start(f32[256,64]{0,1:T(8,128)S(1)} %subtract_subtract_fusion.2), channel_id=1, source_target_pairs={{0,3},{1,0},{2,1},{3,2},{4,7},{5,4},{6,5},{7,6},{8,11},{9,8},{10,9... | collective-permute-start | bytes 196616 | tf_op jit(solution)/shard_map/ppermute | solution.py:17
  593.3 14.1 %collective-permute-start.27 = (f32[256,64]{0,1:T(8,128)S(1)}, f32[256,64]{0,1:T(8,128)S(1)}, u32[]{:S(2)}, u32[]{:S(2)}) collective-permute-start(f32[256,64]{0,1:T(8,128)S(1)} %collective-permute-done.26), channel_id=1, source_target_pairs={{0,1},{1,2},{2,3},{3,0},{4,5},{5,6},{6,7},{7,4},{8,9},{9,10},{10,1... | collective-permute-start | bytes 196616 | tf_op jit(solution)/shard_map/ppermute | solution.py:15
  671.3 12.7 %collective-permute-start.47 = (f32[16,256]{1,0:T(8,128)S(1)}, f32[16,256]{1,0:T(8,128)S(1)}, u32[]{:S(2)}, u32[]{:S(2)}) collective-permute-start(f32[16,256]{1,0:T(8,128)S(1)} %fusion.262), channel_id=1, source_target_pairs={{64,0},{68,4},{72,8},{76,12},{80,16},{84,20},{88,24},{92,28},{96,3... | collective-permute-start | bytes 49160 | tf_op jit(solution)/shard_map/ppermute | solution.py:25
  675.9 8.3 collective-permute-start.30
  679.5 12.1 %collective-permute-start.31 = (f32[256,64]{0,1:T(8,128)S(1)}, f32[256,64]{0,1:T(8,128)S(1)}, u32[]{:S(2)}, u32[]{:S(2)}) collective-permute-start(f32[256,64]{0,1:T(8,128)S(1)} %fusion.263), channel_id=1, source_target_pairs={{64,0},{68,4},{72,8},{76,12},{80,16},{84,20},{88,24},{92,28},{96,3... | collective-permute-start | bytes 196616 | tf_op jit(solution)/shard_map/ppermute | solution.py:25
  681.4 93.5 %collective-permute-start.46 = (f32[16,256]{1,0:T(8,128)}, f32[16,256]{1,0:T(8,128)S(1)}, u32[]{:S(2)}, u32[]{:S(2)}) collective-permute-start(f32[16,256]{1,0:T(8,128)} %fusion.293), channel_id=1, source_target_pairs={{0,64},{4,68},{8,72},{12,76},{16,80},{20,84},{24,88},{28,92},{32,9... | collective-permute-start | bytes 49160 | tf_op jit(solution)/shard_map/ppermute | solution.py:25
  682.7 8.4 collective-permute-start.29
  684.2 6.9 copy-start.3
  691.4 4.3 collective-permute-start.32
  691.8 18.1 %copy-start.4 = (f32[256,64]{0,1:T(8,128)}, f32[256,64]{0,1:T(8,128)S(1)}, u32[]{:S(2)}) copy-start(f32[256,64]{0,1:T(8,128)S(1)} %convolution_negate_fusion.1) | copy-start | bytes 196612
  691.8 18.1 %collective-permute-start.34 = (f32[256,64]{0,1:T(8,128)S(1)}, f32[256,64]{0,1:T(8,128)S(1)}, u32[]{:S(2)}, u32[]{:S(2)}) collective-permute-start(f32[256,64]{0,1:T(8,128)S(1)} %subtract_subtract_fusion.1), channel_id=1, source_target_pairs={{0,3},{1,0},{2,1},{3,2},{4,7},{5,4},{6,5},{7,6},{8,11},{9,8},{10,9... | collective-permute-start | bytes 196616 | tf_op jit(solution)/shard_map/ppermute | solution.py:17
  695.8 14.2 %collective-permute-start.33 = (f32[256,64]{0,1:T(8,128)S(1)}, f32[256,64]{0,1:T(8,128)S(1)}, u32[]{:S(2)}, u32[]{:S(2)}) collective-permute-start(f32[256,64]{0,1:T(8,128)S(1)} %collective-permute-done.32), channel_id=1, source_target_pairs={{0,1},{1,2},{2,3},{3,0},{4,5},{5,6},{6,7},{7,4},{8,9},{9,10},{10,1... | collective-permute-start | bytes 196616 | tf_op jit(solution)/shard_map/ppermute | solution.py:15
  775.2 17.4 %collective-permute-start.49 = (f32[16,256]{1,0:T(8,128)S(1)}, f32[16,256]{1,0:T(8,128)S(1)}, u32[]{:S(2)}, u32[]{:S(2)}) collective-permute-start(f32[16,256]{1,0:T(8,128)S(1)} %fusion.251), channel_id=1, source_target_pairs={{128,0},{132,4},{136,8},{140,12},{144,16},{148,20},{152,24},{156,2... | collective-permute-start | bytes 49160 | tf_op jit(solution)/shard_map/ppermute | solution.py:25
  781.1 11.5 %collective-permute-start.48 = (f32[16,256]{1,0:T(8,128)S(1)}, f32[16,256]{1,0:T(8,128)S(1)}, u32[]{:S(2)}, u32[]{:S(2)}) collective-permute-start(f32[16,256]{1,0:T(8,128)S(1)} %fusion.295), channel_id=1, source_target_pairs={{0,128},{4,132},{8,136},{12,140},{16,144},{20,148},{24,152},{28,15... | collective-permute-start | bytes 49160 | tf_op jit(solution)/shard_map/ppermute | solution.py:25
  782.4 12.3 %collective-permute-start.36 = (f32[256,256]{1,0:T(8,128)S(1)}, f32[256,256]{1,0:T(8,128)S(1)}, u32[]{:S(2)}, u32[]{:S(2)}) collective-permute-start(f32[256,256]{1,0:T(8,128)S(1)} %pad_maximum_fusion.8), channel_id=1, source_target_pairs={{128,0},{132,4},{136,8},{140,12},{144,16},{148,20},{152,24},{156,2... | collective-permute-start | bytes 786440 | tf_op jit(solution)/shard_map/ppermute | solution.py:25
  791.3 10.2 %collective-permute-start.35 = (f32[256,64]{0,1:T(8,128)S(1)}, f32[256,64]{0,1:T(8,128)S(1)}, u32[]{:S(2)}, u32[]{:S(2)}) collective-permute-start(f32[256,64]{0,1:T(8,128)S(1)} %fusion.286), channel_id=1, source_target_pairs={{0,128},{4,132},{8,136},{12,140},{16,144},{20,148},{24,152},{28,15... | collective-permute-start | bytes 196616 | tf_op jit(solution)/shard_map/ppermute | solution.py:25
  851.5 23.9 %copy-start.19 = (f32[256,16]{0,1:T(8,128)S(1)}, f32[256,16]{0,1:T(8,128)}, u32[]{:S(2)}) copy-start(f32[256,16]{0,1:T(8,128)} %subtract_bitcast_fusion) | copy-start | bytes 49156
  876.9 5.1 collective-permute-start.50
  (13 other events, 11.3 us)
